TPU v7x, 256 devices: a whole 4x4x8 slice. The times are simulated.
256 devices in a mesh: cells: 64 (over z, x, core), chan: 4 (over y).
Axes of the slice: x: 4, y: 4, z: 8, core: 2. Of those that a mesh axis runs over, the one named last changes fastest.
Arguments:
- charges: bfloat16 [128, 65536], P('chan', 'cells'), may hold values from -6 to 6
- basis: float32 [25, 65536], P(None, 'cells'), may hold values from -1.5 to 1.5
- atom_leaf: int32 [65536], P('cells'), may hold values from 0 to 8191, as said below
- leaf_lists: int32 [64, 8192], P(None, 'cells'), may hold values from -1 to 8191, as said below
- coarse_lists: int32 [64, 1024], P(None, 'cells'), may hold values from -1 to 1023, as said below
- up_ops: bfloat16 [8, 25, 25], replicated, may hold values from -0.4375 to 0.4375
- down_ops: bfloat16 [8, 25, 25], replicated, may hold values from -1.25 to 1.25
- leaf_ops: bfloat16 [25, 25, 64], replicated, may hold values from -0.15625 to 0.15625
- coarse_ops: bfloat16 [25, 25, 64], replicated, may hold values from -0.15625 to 0.15625
- mix: bfloat16 [128, 128], replicated, may hold values from -0.5 to 0.5
- cotangent: bfloat16 [128, 65536], P('chan', 'cells'), may hold values from -0.005859375 to 0.005859375
Outputs:
- refined: bfloat16 [128, 65536], P('chan', 'cells')
- grad_leaf_ops: float32 [25, 25, 64], replicated
- grad_coarse_ops: float32 [25, 25, 64], replicated
Inputs may be any that keep to these rules, and one draw needn't show every extreme that they name: `atom_leaf`: an atom's leaf is one of the 128 consecutive leaves whose block along cells holds that atom. `leaf_lists`: entry [s, t] is -1 for an empty slot, else a leaf within 64 leaves of the block of 128 leaves that holds t. `coarse_lists`: entry [s, p] is -1 for an empty slot, else a parent cell within 8 cells of the block of 16 parent cells that holds p.
All inputs are finite; a program needn't handle non-finite values.
Results may differ from a plain program's by a relative error of at most 0.014.
Values may be sent and summed in bfloat16 or wider, within the bound.
A program may use at most 128 MiB of HBM per device.

v0:
```python
import jax
import jax.numpy as jnp
from jax import lax
from jax.sharding import PartitionSpec as P

SLOT_BLOCK = 16


def extended(block, sides, width):
    for axis, dim in sides:
        count = lax.axis_size(axis)
        forward = [(i, i + 1) for i in range(count - 1)]
        backward = [(target, source) for source, target in forward]
        low = lax.ppermute(
            lax.slice_in_dim(block, block.shape[dim] - width, None, axis=dim), axis, forward
        )
        high = lax.ppermute(lax.slice_in_dim(block, 0, width, axis=dim), axis, backward)
        block = jnp.concatenate([low, block, high], axis=dim)
    return block


def spread(weights, values, local_leaf, leaf_dev):
    kcount, atoms = weights.shape
    chan_part = values.shape[0]
    width = min(1024, atoms)

    def spread_accumulate(counter, running):
        member = (local_leaf[:, None] == jnp.arange(leaf_dev, dtype=jnp.int32)[None, :]).astype(
            jnp.bfloat16
        )
        scaled = (weights[:, None, :] * values[None].astype(jnp.float32)).astype(jnp.bfloat16)
        return running + jnp.dot(
            scaled.reshape(kcount * chan_part, width), member, preferred_element_type=jnp.float32
        )

    start_value = jnp.zeros((kcount * chan_part, leaf_dev), jnp.float32)
    result = lax.fori_loop(0, atoms // width, spread_accumulate, start_value)
    return result.reshape(kcount, chan_part, leaf_dev)


def collect(weights, fields, local_leaf):
    kcount, chan_part, leaf_dev = fields.shape
    atoms = weights.shape[1]
    width = min(1024, atoms)
    flat_fields = fields.reshape(kcount * chan_part, leaf_dev)

    def collect_accumulate(counter, running):
        member = (jnp.arange(leaf_dev, dtype=jnp.int32)[:, None] == local_leaf[None, :]).astype(
            jnp.bfloat16
        )
        per_atom = jnp.dot(flat_fields, member, preferred_element_type=jnp.float32).reshape(
            kcount, chan_part, width
        )
        summed = jnp.sum(weights[:, None, :] * per_atom, axis=0)
        return summed

    start_value = jnp.zeros((chan_part, atoms), jnp.float32)
    return lax.fori_loop(0, atoms // width, collect_accumulate, start_value)


def pick(source, group_list, first_cell):
    valid = group_list >= 0
    position = jnp.where(valid, group_list - first_cell, 0)
    picked = jnp.take(source, position, axis=2)
    return picked * valid.astype(jnp.bfloat16)[None, None]


def translate(source, lists, first_cell, ops):
    kcount, chan_part, _ = source.shape
    slot_count, targets = lists.shape
    groups = slot_count // SLOT_BLOCK
    list_groups = lists.reshape(groups, SLOT_BLOCK, targets)
    op_groups = jnp.transpose(ops.reshape(kcount, kcount, groups, SLOT_BLOCK), (2, 3, 0, 1))

    def translate_advance(running, pieces):
        group_list, group_ops = pieces
        picked = pick(source, group_list, first_cell)
        return (
            running
            + jnp.einsum("okj,jcot->kct", group_ops, picked, preferred_element_type=jnp.float32),
            None,
        )

    start_value = jnp.zeros((kcount, chan_part, targets), jnp.float32)
    result, _ = lax.scan(translate_advance, start_value, (list_groups, op_groups))
    return result


def slot_gradients(source, lists, first_cell, fields):
    kcount = source.shape[0]
    slot_count, targets = lists.shape
    groups = slot_count // SLOT_BLOCK
    list_groups = lists.reshape(groups, SLOT_BLOCK, targets)

    def slot_advance(carried, group_list):
        picked = pick(source, group_list, first_cell)
        return (
            carried,
            jnp.einsum("kct,jcot->kjo", fields, picked, preferred_element_type=jnp.float32),
        )

    _, stacked = lax.scan(slot_advance, jnp.zeros((), jnp.float32), list_groups)
    return jnp.transpose(stacked, (1, 2, 0, 3)).reshape(kcount, kcount, slot_count)


def local(
    charges,
    basis,
    atom_leaf,
    leaf_lists,
    coarse_lists,
    up_ops,
    down_ops,
    leaf_ops,
    coarse_ops,
    mix,
    cotangent,
):
    chan_part = charges.shape[0]
    kcount = basis.shape[0]
    leaf_dev = leaf_lists.shape[1]
    coarse_dev = coarse_lists.shape[1]
    cells_pos = lax.axis_index("cells")
    chan_pos = lax.axis_index("chan")
    local_leaf = atom_leaf - cells_pos * leaf_dev
    moments = spread(basis, charges, local_leaf, leaf_dev).astype(jnp.bfloat16)
    grouped = moments.reshape(kcount, chan_part, coarse_dev, 8)
    coarse = jnp.einsum(
        "okj,jcpo->kcp", up_ops, grouped, preferred_element_type=jnp.float32
    ).astype(jnp.bfloat16)
    leaf_source = extended(moments, (("cells", 2),), leaf_dev // 2)
    leaf_first = cells_pos * leaf_dev - leaf_dev // 2
    coarse_source = extended(coarse, (("cells", 2),), coarse_dev // 2)
    coarse_first = cells_pos * coarse_dev - coarse_dev // 2
    near_field = translate(leaf_source, leaf_lists, leaf_first, leaf_ops)
    far_field = translate(coarse_source, coarse_lists, coarse_first, coarse_ops).astype(
        jnp.bfloat16
    )
    child = jnp.einsum("okj,jcp->kcpo", down_ops, far_field, preferred_element_type=jnp.float32)
    expansion = (near_field + child.reshape(kcount, chan_part, leaf_dev)).astype(jnp.bfloat16)
    potential = collect(basis, expansion, local_leaf).astype(jnp.bfloat16)
    rows_mine = lax.dynamic_slice_in_dim(mix, chan_pos * chan_part, chan_part, 0)
    cols_mine = lax.dynamic_slice_in_dim(mix, chan_pos * chan_part, chan_part, 1)
    mixed = lax.dot_general(
        cols_mine,
        lax.all_gather(potential, "chan", axis=0, tiled=True),
        (((0,), (0,)), ((), ())),
        preferred_element_type=jnp.float32,
    )
    back_sum = jnp.dot(
        rows_mine,
        lax.all_gather(cotangent, "chan", axis=0, tiled=True),
        preferred_element_type=jnp.float32,
    )
    refined = (charges.astype(jnp.float32) + mixed).astype(jnp.bfloat16)
    back_potential = back_sum.astype(jnp.bfloat16)
    back_expansion = spread(basis, back_potential, local_leaf, leaf_dev).astype(jnp.bfloat16)
    back_grouped = back_expansion.reshape(kcount, chan_part, coarse_dev, 8)
    back_far = jnp.einsum(
        "okj,kcpo->jcp", down_ops, back_grouped, preferred_element_type=jnp.float32
    ).astype(jnp.bfloat16)
    grad_leaf = slot_gradients(leaf_source, leaf_lists, leaf_first, back_expansion)
    grad_coarse = slot_gradients(coarse_source, coarse_lists, coarse_first, back_far)
    grad_leaf, grad_coarse = lax.psum((grad_leaf, grad_coarse), ("cells", "chan"))
    return (refined, grad_leaf, grad_coarse)


def solution(mesh):
    placed = (
        P("chan", "cells"),
        P(None, "cells"),
        P("cells"),
        P(None, "cells"),
        P(None, "cells"),
        P(),
        P(),
        P(),
        P(),
        P(),
        P("chan", "cells"),
    )
    return jax.shard_map(
        local, mesh=mesh, in_specs=placed, out_specs=(P("chan", "cells"), P(), P()), check_vma=False
    )
```

profile of v0, /device:TPU:2, one launch (start us, length us, event | category | flops | bytes accessed | tf_op | source)
XLA Modules:
  0.0 724.2 jit_solution(9109661945923828574)
XLA Ops:
  8.8 1.6 fusion.47
  11.2 1.9 collective-permute-start.1
  13.2 2.4 collective-permute-start
  15.6 1.7 copy.72
  17.7 3.8 collective-permute-start.3
  21.5 1.9 collective-permute-start.2
  23.4 12.3 %all_gather.7 = bf16[128,1024]{1,0:T(8,128)(2,1)S(1)} all-gather(bf16[32,1024]{1,0:T(8,128)(2,1)S(1)} %copy-done.9), channel_id=1, replica_groups=mesh['cells'=64,'chan'=4] {'chan'}, dimensions={0}, use_global_device_ids=true | all-gather | bytes 327680 | tf_op jit(solution)/shard_map/all_gather | solution.py:152
  36.7 1.7 copy.75
  39.5 1.7 copy.40
  43.4 13.1 %while.57 = (s32[]{:T(128)}, f32[25,32,16]{1,0,2:T(8,128)S(1)}, bf16[4,16,25,25]{3,2,1,0:T(8,128)(2,1)S(1)}, s32[4,16,16]{2,1,0:T(8,128)S(1)}, s32[]{:T(128)}, /...) while((s32[]{:T(128)}, f32[25,32,16]{1,0,2:T(8,128)S(1)}, ...), condition=%wide.region_3.6_spmd.clone, body=%wide.region_2.5_spmd.clone.sunk | while | flops 10678787 | bytes 4553847 | solution.py:85
  43.8 1.0 gather_fusion.3
  45.7 1.2 fusion.101
  47.0 1.0 gather_fusion.3
  48.9 1.2 fusion.101
  50.3 1.0 gather_fusion.3
  52.2 1.2 fusion.101
  53.5 1.0 gather_fusion.3
  55.4 1.2 fusion.101
  56.6 17.5 %while.15 = (s32[]{:T(128)}, f32[4,25,25,16]{1,2,3,0:T(8,128)}, s32[4,16,16]{2,1,0:T(8,128)S(1)}, s32[]{:T(128)}, bf16[25,32,32]{1,0,2:T(8,128)(2,1)S(1)}, /*index=5*/bf16[25,32,16]{1,0,2:T(8,128)(2,1)}, s32[]{:T(128)}) while((s32[]{:T(128)}, f32[4,25,25,16]{1,2,3,0:T(8,128)}, s32[4,16,16]{2,1,0:T(8,128)S(1)}, s32[]{:T(128)}, ...), condition=%wide.region_9.12_spmd, body=%wide.region_8.11_spmd.sunk | while | flops 10653186 | bytes 3270785 | solution.py:102
  56.7 1.0 gather_fusion.1
  59.3 1.7 fusion.96
  61.1 1.0 gather_fusion.1
  63.7 1.7 fusion.96
  65.5 1.0 gather_fusion.1
  68.0 1.7 fusion.96
  69.9 1.0 gather_fusion.1
  72.4 1.7 fusion.96
  74.6 1.3 copy.50
  75.9 2.9 copy.61
  78.9 1.3 pad_maximum_fusion
  80.2 3.0 copy.41
  83.2 193.7 %while.56 = (s32[]{:T(128)}, f32[25,32,128]{2,0,1:T(8,128)}, bf16[4,16,25,25]{3,2,1,0:T(8,128)(2,1)}, s32[4,16,128]{2,1,0:T(8,128)S(1)}, s32[]{:T(128)}, /*index...) while((s32[]{:T(128)}, f32[25,32,128]{2,0,1:T(8,128)}, bf16[4,16,25,25]{3,2,1,0:T(8,128)(2,1)}, ...), condition=%wide.region_1.3_spmd.clone, body=%wide.region_0.2_spmd.clone.sunk | while | flops 90349568 | bytes 18425984 | solution.py:85
  83.2 19.3 %gather_fusion.2 = bf16[2048,25,32]{2,1,0:T(8,128)(2,1)} fusion(bf16[25,32,256]{1,0,2:T(8,128)(2,1)S(1)} %get-tuple-element.527, s32[2048]{0:T(1024)S(1)} %bitcast_clamp_fusion.5), kind=kCustom, calls=%fused_computation.clone.clone.1 | custom fusion | bytes 6561792 | tf_op jit(solution)/shard_map/while/body/eval_jaxpr/jit(_take)/gather | solution.py:64
  102.5 24.5 %copy.113 = bf16[16,128,25,32]{1,2,0,3:T(8,128)(2,1)} copy(bf16[16,128,25,32]{3,2,1,0:T(8,128)(2,1)} %bitcast.208) | data formatting | bytes 6553600 | tf_op jit(solution)/shard_map/while/body/eval_jaxpr/jit(_take)/gather | solution.py:64
  127.1 4.5 fusion.98
  131.5 19.3 %gather_fusion.2 = bf16[2048,25,32]{2,1,0:T(8,128)(2,1)} fusion(bf16[25,32,256]{1,0,2:T(8,128)(2,1)S(1)} %get-tuple-element.527, s32[2048]{0:T(1024)S(1)} %bitcast_clamp_fusion.5), kind=kCustom, calls=%fused_computation.clone.clone.1 | custom fusion | bytes 6561792 | tf_op jit(solution)/shard_map/while/body/eval_jaxpr/jit(_take)/gather | solution.py:64
  150.8 24.5 %copy.113 = bf16[16,128,25,32]{1,2,0,3:T(8,128)(2,1)} copy(bf16[16,128,25,32]{3,2,1,0:T(8,128)(2,1)} %bitcast.208) | data formatting | bytes 6553600 | tf_op jit(solution)/shard_map/while/body/eval_jaxpr/jit(_take)/gather | solution.py:64
  175.4 4.6 fusion.98
  180.0 19.3 %gather_fusion.2 = bf16[2048,25,32]{2,1,0:T(8,128)(2,1)} fusion(bf16[25,32,256]{1,0,2:T(8,128)(2,1)S(1)} %get-tuple-element.527, s32[2048]{0:T(1024)S(1)} %bitcast_clamp_fusion.5), kind=kCustom, calls=%fused_computation.clone.clone.1 | custom fusion | bytes 6561792 | tf_op jit(solution)/shard_map/while/body/eval_jaxpr/jit(_take)/gather | solution.py:64
  199.3 24.5 %copy.113 = bf16[16,128,25,32]{1,2,0,3:T(8,128)(2,1)} copy(bf16[16,128,25,32]{3,2,1,0:T(8,128)(2,1)} %bitcast.208) | data formatting | bytes 6553600 | tf_op jit(solution)/shard_map/while/body/eval_jaxpr/jit(_take)/gather | solution.py:64
  223.8 4.6 fusion.98
  228.4 19.3 %gather_fusion.2 = bf16[2048,25,32]{2,1,0:T(8,128)(2,1)} fusion(bf16[25,32,256]{1,0,2:T(8,128)(2,1)S(1)} %get-tuple-element.527, s32[2048]{0:T(1024)S(1)} %bitcast_clamp_fusion.5), kind=kCustom, calls=%fused_computation.clone.clone.1 | custom fusion | bytes 6561792 | tf_op jit(solution)/shard_map/while/body/eval_jaxpr/jit(_take)/gather | solution.py:64
  247.7 24.5 %copy.113 = bf16[16,128,25,32]{1,2,0,3:T(8,128)(2,1)} copy(bf16[16,128,25,32]{3,2,1,0:T(8,128)(2,1)} %bitcast.208) | data formatting | bytes 6553600 | tf_op jit(solution)/shard_map/while/body/eval_jaxpr/jit(_take)/gather | solution.py:64
  272.2 4.6 fusion.98
  276.8 1.2 add_convert_fusion
  278.6 12.3 %all_gather.6 = bf16[128,1024]{1,0:T(8,128)(2,1)S(1)} all-gather(bf16[32,1024]{1,0:T(8,128)(2,1)S(1)} %multiply_reduce_fusion), channel_id=1, replica_groups=mesh['cells'=64,'chan'=4] {'chan'}, dimensions={0}, use_global_device_ids=true | all-gather | bytes 327680 | tf_op jit(solution)/shard_map/all_gather | solution.py:146
  290.9 151.2 %while.14 = (s32[]{:T(128)}, f32[4,25,25,16]{1,3,2,0:T(8,128)}, s32[4,16,128]{2,1,0:T(8,128)S(1)}, s32[]{:T(128)}, bf16[25,32,256]{1,0,2:T(8,128)(2,1)S(1)}, /*index=5*/bf16[25,32,128]{2,0,1:T(8,128)(2,1)S(1)}, s32[]{:T(128)}) while((s32[]{:T(128)}, f32[4,25,25,16]{1,3,2,0:T(8,128)}, s32[4,16,128]{2,1,0:T(8,128)S(1)}, s32[]{:T(128)}, ...), condition=%wide.region_6.9_spmd, body=%wide.region_5.8_spmd.sunk | while | flops 85229568 | bytes 16853100 | solution.py:102
  290.9 19.3 %gather_fusion = bf16[2048,25,32]{2,1,0:T(8,128)(2,1)} fusion(bf16[25,32,256]{1,0,2:T(8,128)(2,1)S(1)} %get-tuple-element.572, s32[2048]{0:T(1024)S(1)} %bitcast_clamp_fusion.4), kind=kCustom, calls=%fused_computation.2.clone.clone.1 | custom fusion | bytes 6561792 | tf_op jit(solution)/shard_map/while/body/eval_jaxpr/jit(_take)/gather | solution.py:64
  310.2 14.9 %copy.110 = bf16[16,128,25,32]{1,0,3,2:T(8,128)(2,1)} copy(bf16[16,128,25,32]{3,2,1,0:T(8,128)(2,1)} %bitcast.209) | data formatting | bytes 6553600 | tf_op jit(solution)/shard_map/while/body/eval_jaxpr/jit(_take)/gather | solution.py:64
  325.1 3.6 fusion.93
  328.7 19.3 %gather_fusion = bf16[2048,25,32]{2,1,0:T(8,128)(2,1)} fusion(bf16[25,32,256]{1,0,2:T(8,128)(2,1)S(1)} %get-tuple-element.572, s32[2048]{0:T(1024)S(1)} %bitcast_clamp_fusion.4), kind=kCustom, calls=%fused_computation.2.clone.clone.1 | custom fusion | bytes 6561792 | tf_op jit(solution)/shard_map/while/body/eval_jaxpr/jit(_take)/gather | solution.py:64
  348.0 14.9 %copy.110 = bf16[16,128,25,32]{1,0,3,2:T(8,128)(2,1)} copy(bf16[16,128,25,32]{3,2,1,0:T(8,128)(2,1)} %bitcast.209) | data formatting | bytes 6553600 | tf_op jit(solution)/shard_map/while/body/eval_jaxpr/jit(_take)/gather | solution.py:64
  362.9 3.6 fusion.93
  366.5 19.3 %gather_fusion = bf16[2048,25,32]{2,1,0:T(8,128)(2,1)} fusion(bf16[25,32,256]{1,0,2:T(8,128)(2,1)S(1)} %get-tuple-element.572, s32[2048]{0:T(1024)S(1)} %bitcast_clamp_fusion.4), kind=kCustom, calls=%fused_computation.2.clone.clone.1 | custom fusion | bytes 6561792 | tf_op jit(solution)/shard_map/while/body/eval_jaxpr/jit(_take)/gather | solution.py:64
  385.8 14.9 %copy.110 = bf16[16,128,25,32]{1,0,3,2:T(8,128)(2,1)} copy(bf16[16,128,25,32]{3,2,1,0:T(8,128)(2,1)} %bitcast.209) | data formatting | bytes 6553600 | tf_op jit(solution)/shard_map/while/body/eval_jaxpr/jit(_take)/gather | solution.py:64
  400.7 3.6 fusion.93
  404.3 19.3 %gather_fusion = bf16[2048,25,32]{2,1,0:T(8,128)(2,1)} fusion(bf16[25,32,256]{1,0,2:T(8,128)(2,1)S(1)} %get-tuple-element.572, s32[2048]{0:T(1024)S(1)} %bitcast_clamp_fusion.4), kind=kCustom, calls=%fused_computation.2.clone.clone.1 | custom fusion | bytes 6561792 | tf_op jit(solution)/shard_map/while/body/eval_jaxpr/jit(_take)/gather | solution.py:64
  423.6 14.9 %copy.110 = bf16[16,128,25,32]{1,0,3,2:T(8,128)(2,1)} copy(bf16[16,128,25,32]{3,2,1,0:T(8,128)(2,1)} %bitcast.209) | data formatting | bytes 6553600 | tf_op jit(solution)/shard_map/while/body/eval_jaxpr/jit(_take)/gather | solution.py:64
  438.5 3.6 fusion.93
  442.1 2.9 copy.54
  445.0 0.9 fusion.52
  445.9 267.0 %all-reduce.3.cloned.1.call-done = (f32[25,25,64]{1,2,0:T(8,128)}, f32[25,25,64]{1,2,0:T(8,128)}) async-done(((f32[25,25,64]{1,2,0:T(8,128)}, f32[25,25,64]{1,2,0:T(8,128)}), (f32[25,25,64]{1,2,0:T(8,128)}, f32[25,25,64]{1,2,0:T(8,128)})) %all-reduce.3.cloned.1.call-update) | async-done | bytes 320016 | tf_op jit(solution)/shard_map/psum | solution.py:164
  712.9 2.2 copy.62
  715.1 2.2 copy.63
  (130 shorter events, 19.1 us)
Async XLA Ops:
  7.2 28.6 %copy-start = (bf16[128,128]{1,0:T(8,128)(2,1)S(1)}, bf16[128,128]{1,0:T(8,128)(2,1)}, u32[]{:S(2)}) copy-start(bf16[128,128]{1,0:T(8,128)(2,1)} %param.32) | copy-start | bytes 98308
  7.2 705.7 %all-reduce.3.cloned.1.call-start = ((), (), s32[]{:S(2)}) async-start(), calls=%async_computation | async-start | bytes 3276800 | tf_op jit(solution)/shard_map/psum | solution.py:164
  8.1 9.2 %copy-start.7 = (bf16[8,25,25]{2,0,1:T(8,128)(2,1)S(1)}, bf16[8,25,25]{2,0,1:T(8,128)(2,1)}, u32[]{:S(2)}) copy-start(bf16[8,25,25]{2,0,1:T(8,128)(2,1)} %param.28) | copy-start | bytes 30004
  10.4 13.0 %copy-start.9 = (bf16[32,1024]{1,0:T(8,128)(2,1)S(1)}, bf16[32,1024]{1,0:T(8,128)(2,1)}, u32[]{:S(2)}) copy-start(bf16[32,1024]{1,0:T(8,128)(2,1)} %param.33) | copy-start | bytes 196612
  10.4 25.5 %copy-start.11 = (f32[25,1024]{1,0:T(8,128)S(1)}, f32[25,1024]{1,0:T(8,128)}, u32[]{:S(2)}) copy-start(f32[25,1024]{1,0:T(8,128)} %param.24) | copy-start | bytes 307204
  11.2 67.6 %collective-permute-start.1 = (bf16[25,32,64]{2,1,0:T(8,128)(2,1)}, bf16[25,32,64]{2,1,0:T(8,128)(2,1)}, u32[]{:S(2)}, u32[]{:S(2)}) collective-permute-start(bf16[25,32,64]{2,1,0:T(8,128)(2,1)} %get-tuple-element.331), channel_id=1, source_target_pairs={{4,0},{8,4},{12,8},{16,12},{20,16},{24,20},{28,24},{32,28},{36,32}... | collective-permute-start | bytes 307208 | tf_op jit(solution)/shard_map/ppermute | solution.py:17
  13.2 65.7 %collective-permute-start = (bf16[25,32,64]{2,1,0:T(8,128)(2,1)}, bf16[25,32,64]{2,1,0:T(8,128)(2,1)}, u32[]{:S(2)}, u32[]{:S(2)}) collective-permute-start(bf16[25,32,64]{2,1,0:T(8,128)(2,1)} %get-tuple-element.330), channel_id=1, source_target_pairs={{0,4},{4,8},{8,12},{12,16},{16,20},{20,24},{24,28},{28,32},{32,36}... | collective-permute-start | bytes 307208 | tf_op jit(solution)/shard_map/ppermute | solution.py:14
  17.7 20.6 %copy-start.8 = (bf16[8,25,25]{2,0,1:T(8,128)(2,1)S(1)}, bf16[8,25,25]{2,0,1:T(8,128)(2,1)}, u32[]{:S(2)}) copy-start(bf16[8,25,25]{2,0,1:T(8,128)(2,1)} %param.29) | copy-start | bytes 30004
  17.7 25.4 %collective-permute-start.3 = (bf16[25,32,8]{0,1,2:T(8,128)(2,1)S(1)}, bf16[25,32,8]{0,1,2:T(8,128)(2,1)S(1)}, u32[]{:S(2)}, u32[]{:S(2)}) collective-permute-start(bf16[25,32,8]{0,1,2:T(8,128)(2,1)S(1)} %get-tuple-element.333), channel_id=1, source_target_pairs={{4,0},{8,4},{12,8},{16,12},{20,16},{24,20},{28,24},{32,28},{36,32}... | collective-permute-start | bytes 38408 | tf_op jit(solution)/shard_map/ppermute | solution.py:17
  21.5 21.6 %collective-permute-start.2 = (bf16[25,32,8]{0,1,2:T(8,128)(2,1)S(1)}, bf16[25,32,8]{0,1,2:T(8,128)(2,1)S(1)}, u32[]{:S(2)}, u32[]{:S(2)}) collective-permute-start(bf16[25,32,8]{0,1,2:T(8,128)(2,1)S(1)} %get-tuple-element.332), channel_id=1, source_target_pairs={{0,4},{4,8},{8,12},{12,16},{16,20},{20,24},{24,28},{28,32},{32,36}... | collective-permute-start | bytes 38408 | tf_op jit(solution)/shard_map/ppermute | solution.py:14
  35.9 3.6 copy-start.4
  36.6 4.6 copy-start.5
  36.6 5.5 copy-start.10
  58.4 0.9 copy-start.6
  62.8 0.9 copy-start.6
  67.1 0.9 copy-start.6
  71.5 0.9 copy-start.6
  78.9 4.3 copy-start.1
  83.2 194.9 %copy-start.12 = (f32[25,1024]{1,0:T(8,128)S(1)}, f32[25,1024]{1,0:T(8,128)}, u32[]{:S(2)}) copy-start(f32[25,1024]{1,0:T(8,128)} %param.24) | copy-start | bytes 307204
  276.8 14.1 %copy-start.2 = (bf16[25,32,128]{2,0,1:T(8,128)(2,1)S(1)}, bf16[25,32,128]{2,0,1:T(8,128)(2,1)}, u32[]{:S(2)}) copy-start(bf16[25,32,128]{2,0,1:T(8,128)(2,1)} %copy.53) | copy-start | bytes 614404
  442.1 2.9 copy-start.3
Sparse Core Ops, SparseCore 0:
  445.1 267.7 all-reduce.2
where the time goes:
time: 726 us; the launch traced here: 724 us
  local copies, waits for them, and re-layouts  352 us (48%)
  waiting for transfers between devices  267 us (37%)
  matrix products  49.3 us (7%)
  blocking collectives  24.6 us (3%)
  between operations  14.3 us (2%)
  starting transfers between devices  10 us (1%)
    gather x32, local copies, waits for them, and re-layouts, pick(): picked = jnp.take(source, position, axis=2)  325 us
    psum x1, waiting for transfers between devices, local(): lax.psum((grad_leaf, grad_coarse), ('cells', 'chan'))  267 us
    dot_general x8, matrix products, translate_advance(): jnp.einsum('okj,jcot->kct', group_ops, picked, preferred_element_type=jnp...  22.9 us
    dot_general x8, matrix products, slot_advance(): jnp.einsum('kct,jcot->kjo', fields, picked, preferred_element_type=jnp.fl...  21.2 us
  transfers between devices with their start and end apart: 5, of which 1 were waited for; matrix products, arithmetic and copies ran while one was open for 6% of the time, Pallas kernels for 0%

commit v1 on v0

--- a/solution.py
+++ b/solution.py
@@ -161,7 +161,7 @@
     ).astype(jnp.bfloat16)
     grad_leaf = slot_gradients(leaf_source, leaf_lists, leaf_first, back_expansion)
     grad_coarse = slot_gradients(coarse_source, coarse_lists, coarse_first, back_far)
-    grad_leaf, grad_coarse = lax.psum((grad_leaf, grad_coarse), ("cells", "chan"))
+    grad_leaf, grad_coarse = lax.psum(lax.psum((grad_leaf, grad_coarse), "chan"), "cells")
     return (refined, grad_leaf, grad_coarse)
 
 

time: 726 us -> 697 us (0.960)
  waiting for transfers between devices: 267 us -> 239 us
    psum x1 -> x2, waiting for transfers between devices: 267 us -> 239 us  [the longest x1 190 us: local(): lax.psum(lax.psum((grad_leaf, grad_coarse), 'chan'), 'cells')]
  transfers between devices with their start and end apart: 5 -> 6, of which waited for: 1 -> 2; matrix products, arithmetic and copies ran while one was open for 6% -> 6% of each run, Pallas kernels for 0% -> 0%
where the time goes in v1:
time: 697 us; the launch traced here: 695 us
  local copies, waits for them, and re-layouts  351 us (50%)
  waiting for transfers between devices  239 us (34%)
  matrix products  49.2 us (7%)
  blocking collectives  24.6 us (4%)
  between operations  14.4 us (2%)
  starting transfers between devices  10.1 us (1%)
    gather x32, local copies, waits for them, and re-layouts, pick(): picked = jnp.take(source, position, axis=2)  325 us
    psum x1, waiting for transfers between devices, local(): lax.psum(lax.psum((grad_leaf, grad_coarse), 'chan'), 'cells')  190 us
    psum x1, waiting for transfers between devices, local(): lax.psum((grad_leaf, grad_coarse), 'chan')  48.4 us
    dot_general x8, matrix products, translate_advance(): jnp.einsum('okj,jcot->kct', group_ops, picked, preferred_element_type=jnp...  22.8 us
    dot_general x8, matrix products, slot_advance(): jnp.einsum('kct,jcot->kjo', fields, picked, preferred_element_type=jnp.fl...  21.2 us
  transfers between devices with their start and end apart: 6, of which 2 were waited for; matrix products, arithmetic and copies ran while one was open for 6% of the time, Pallas kernels for 0%

profile of v1, /device:TPU:2, one launch (start us, length us, event | category | flops | bytes accessed | tf_op | source)
XLA Modules:
  0.0 694.5 jit_solution(4402984464782514003)
XLA Ops:
  8.8 1.6 fusion.47
  11.3 1.9 collective-permute-start.1
  13.2 2.4 collective-permute-start
  15.6 1.7 copy.72
  17.7 3.8 collective-permute-start.3
  21.5 1.9 collective-permute-start.2
  23.5 12.3 %all_gather.7 = bf16[128,1024]{1,0:T(8,128)(2,1)S(1)} all-gather(bf16[32,1024]{1,0:T(8,128)(2,1)S(1)} %copy-done.10), channel_id=1, replica_groups=mesh['cells'=64,'chan'=4] {'chan'}, dimensions={0}, use_global_device_ids=true | all-gather | bytes 327680 | tf_op jit(solution)/shard_map/all_gather | solution.py:152
  36.7 1.7 copy.75
  39.6 1.7 copy.40
  43.4 13.1 %while.57 = (s32[]{:T(128)}, f32[25,32,16]{1,0,2:T(8,128)S(1)}, bf16[4,16,25,25]{3,2,1,0:T(8,128)(2,1)S(1)}, s32[4,16,16]{2,1,0:T(8,128)S(1)}, s32[]{:T(128)}, /...) while((s32[]{:T(128)}, f32[25,32,16]{1,0,2:T(8,128)S(1)}, ...), condition=%wide.region_3.6_spmd.clone, body=%wide.region_2.5_spmd.clone.sunk | while | flops 10678787 | bytes 4553847 | solution.py:85
  43.8 1.0 gather_fusion.3
  45.7 1.2 fusion.101
  47.0 1.0 gather_fusion.3
  48.9 1.2 fusion.101
  50.3 1.0 gather_fusion.3
  52.2 1.2 fusion.101
  53.5 1.0 gather_fusion.3
  55.4 1.2 fusion.101
  56.6 17.5 %while.15 = (s32[]{:T(128)}, f32[4,25,25,16]{1,2,3,0:T(8,128)}, s32[4,16,16]{2,1,0:T(8,128)S(1)}, s32[]{:T(128)}, bf16[25,32,32]{1,0,2:T(8,128)(2,1)S(1)}, /*index=5*/bf16[25,32,16]{1,0,2:T(8,128)(2,1)}, s32[]{:T(128)}) while((s32[]{:T(128)}, f32[4,25,25,16]{1,2,3,0:T(8,128)}, s32[4,16,16]{2,1,0:T(8,128)S(1)}, s32[]{:T(128)}, ...), condition=%wide.region_10.13_spmd, body=%wide.region_9.12_spmd.sunk | while | flops 10653186 | bytes 3270785 | solution.py:102
  56.7 1.0 gather_fusion.1
  59.3 1.7 fusion.96
  61.1 1.0 gather_fusion.1
  63.7 1.7 fusion.96
  65.5 1.0 gather_fusion.1
  68.0 1.7 fusion.96
  69.8 1.0 gather_fusion.1
  72.4 1.7 fusion.96
  74.6 1.3 copy.50
  75.9 2.9 copy.61
  78.8 1.3 pad_maximum_fusion
  80.1 3.0 copy.41
  83.1 193.5 %while.56 = (s32[]{:T(128)}, f32[25,32,128]{2,0,1:T(8,128)}, bf16[4,16,25,25]{3,2,1,0:T(8,128)(2,1)}, s32[4,16,128]{2,1,0:T(8,128)S(1)}, s32[]{:T(128)}, /*index...) while((s32[]{:T(128)}, f32[25,32,128]{2,0,1:T(8,128)}, bf16[4,16,25,25]{3,2,1,0:T(8,128)(2,1)}, ...), condition=%wide.region_1.3_spmd.clone, body=%wide.region_0.2_spmd.clone.sunk | while | flops 90349568 | bytes 18425984 | solution.py:85
  83.2 19.2 %gather_fusion.2 = bf16[2048,25,32]{2,1,0:T(8,128)(2,1)} fusion(bf16[25,32,256]{1,0,2:T(8,128)(2,1)S(1)} %get-tuple-element.529, s32[2048]{0:T(1024)S(1)} %bitcast_clamp_fusion.5), kind=kCustom, calls=%fused_computation.clone.clone.1 | custom fusion | bytes 6561792 | tf_op jit(solution)/shard_map/while/body/eval_jaxpr/jit(_take)/gather | solution.py:64
  102.4 24.6 %copy.113 = bf16[16,128,25,32]{1,2,0,3:T(8,128)(2,1)} copy(bf16[16,128,25,32]{3,2,1,0:T(8,128)(2,1)} %bitcast.208) | data formatting | bytes 6553600 | tf_op jit(solution)/shard_map/while/body/eval_jaxpr/jit(_take)/gather | solution.py:64
  127.0 4.5 fusion.98
  131.5 19.2 %gather_fusion.2 = bf16[2048,25,32]{2,1,0:T(8,128)(2,1)} fusion(bf16[25,32,256]{1,0,2:T(8,128)(2,1)S(1)} %get-tuple-element.529, s32[2048]{0:T(1024)S(1)} %bitcast_clamp_fusion.5), kind=kCustom, calls=%fused_computation.clone.clone.1 | custom fusion | bytes 6561792 | tf_op jit(solution)/shard_map/while/body/eval_jaxpr/jit(_take)/gather | solution.py:64
  150.7 24.6 %copy.113 = bf16[16,128,25,32]{1,2,0,3:T(8,128)(2,1)} copy(bf16[16,128,25,32]{3,2,1,0:T(8,128)(2,1)} %bitcast.208) | data formatting | bytes 6553600 | tf_op jit(solution)/shard_map/while/body/eval_jaxpr/jit(_take)/gather | solution.py:64
  175.3 4.6 fusion.98
  179.8 19.2 %gather_fusion.2 = bf16[2048,25,32]{2,1,0:T(8,128)(2,1)} fusion(bf16[25,32,256]{1,0,2:T(8,128)(2,1)S(1)} %get-tuple-element.529, s32[2048]{0:T(1024)S(1)} %bitcast_clamp_fusion.5), kind=kCustom, calls=%fused_computation.clone.clone.1 | custom fusion | bytes 6561792 | tf_op jit(solution)/shard_map/while/body/eval_jaxpr/jit(_take)/gather | solution.py:64
  199.1 24.6 %copy.113 = bf16[16,128,25,32]{1,2,0,3:T(8,128)(2,1)} copy(bf16[16,128,25,32]{3,2,1,0:T(8,128)(2,1)} %bitcast.208) | data formatting | bytes 6553600 | tf_op jit(solution)/shard_map/while/body/eval_jaxpr/jit(_take)/gather | solution.py:64
  223.7 4.6 fusion.98
  228.2 19.2 %gather_fusion.2 = bf16[2048,25,32]{2,1,0:T(8,128)(2,1)} fusion(bf16[25,32,256]{1,0,2:T(8,128)(2,1)S(1)} %get-tuple-element.529, s32[2048]{0:T(1024)S(1)} %bitcast_clamp_fusion.5), kind=kCustom, calls=%fused_computation.clone.clone.1 | custom fusion | bytes 6561792 | tf_op jit(solution)/shard_map/while/body/eval_jaxpr/jit(_take)/gather | solution.py:64
  247.5 24.6 %copy.113 = bf16[16,128,25,32]{1,2,0,3:T(8,128)(2,1)} copy(bf16[16,128,25,32]{3,2,1,0:T(8,128)(2,1)} %bitcast.208) | data formatting | bytes 6553600 | tf_op jit(solution)/shard_map/while/body/eval_jaxpr/jit(_take)/gather | solution.py:64
  272.1 4.6 fusion.98
  276.6 150.9 %while.14 = (s32[]{:T(128)}, f32[4,25,25,16]{1,3,2,0:T(8,128)}, s32[4,16,128]{2,1,0:T(8,128)S(1)}, s32[]{:T(128)}, bf16[25,32,256]{1,0,2:T(8,128)(2,1)S(1)}, /*index=5*/bf16[25,32,128]{2,0,1:T(8,128)(2,1)S(1)}, s32[]{:T(128)}) while((s32[]{:T(128)}, f32[4,25,25,16]{1,3,2,0:T(8,128)}, s32[4,16,128]{2,1,0:T(8,128)S(1)}, s32[]{:T(128)}, ...), condition=%wide.region_6.9_spmd, body=%wide.region_5.8_spmd.sunk | while | flops 85229568 | bytes 16853100 | solution.py:102
  276.6 19.2 %gather_fusion = bf16[2048,25,32]{2,1,0:T(8,128)(2,1)} fusion(bf16[25,32,256]{1,0,2:T(8,128)(2,1)S(1)} %get-tuple-element.574, s32[2048]{0:T(1024)S(1)} %bitcast_clamp_fusion.4), kind=kCustom, calls=%fused_computation.2.clone.clone.1 | custom fusion | bytes 6561792 | tf_op jit(solution)/shard_map/while/body/eval_jaxpr/jit(_take)/gather | solution.py:64
  295.9 14.9 %copy.110 = bf16[16,128,25,32]{1,0,3,2:T(8,128)(2,1)} copy(bf16[16,128,25,32]{3,2,1,0:T(8,128)(2,1)} %bitcast.209) | data formatting | bytes 6553600 | tf_op jit(solution)/shard_map/while/body/eval_jaxpr/jit(_take)/gather | solution.py:64
  310.8 3.6 fusion.93
  314.4 19.2 %gather_fusion = bf16[2048,25,32]{2,1,0:T(8,128)(2,1)} fusion(bf16[25,32,256]{1,0,2:T(8,128)(2,1)S(1)} %get-tuple-element.574, s32[2048]{0:T(1024)S(1)} %bitcast_clamp_fusion.4), kind=kCustom, calls=%fused_computation.2.clone.clone.1 | custom fusion | bytes 6561792 | tf_op jit(solution)/shard_map/while/body/eval_jaxpr/jit(_take)/gather | solution.py:64
  333.6 14.9 %copy.110 = bf16[16,128,25,32]{1,0,3,2:T(8,128)(2,1)} copy(bf16[16,128,25,32]{3,2,1,0:T(8,128)(2,1)} %bitcast.209) | data formatting | bytes 6553600 | tf_op jit(solution)/shard_map/while/body/eval_jaxpr/jit(_take)/gather | solution.py:64
  348.5 3.6 fusion.93
  352.1 19.2 %gather_fusion = bf16[2048,25,32]{2,1,0:T(8,128)(2,1)} fusion(bf16[25,32,256]{1,0,2:T(8,128)(2,1)S(1)} %get-tuple-element.574, s32[2048]{0:T(1024)S(1)} %bitcast_clamp_fusion.4), kind=kCustom, calls=%fused_computation.2.clone.clone.1 | custom fusion | bytes 6561792 | tf_op jit(solution)/shard_map/while/body/eval_jaxpr/jit(_take)/gather | solution.py:64
  371.4 14.9 %copy.110 = bf16[16,128,25,32]{1,0,3,2:T(8,128)(2,1)} copy(bf16[16,128,25,32]{3,2,1,0:T(8,128)(2,1)} %bitcast.209) | data formatting | bytes 6553600 | tf_op jit(solution)/shard_map/while/body/eval_jaxpr/jit(_take)/gather | solution.py:64
  386.2 3.6 fusion.93
  389.8 19.2 %gather_fusion = bf16[2048,25,32]{2,1,0:T(8,128)(2,1)} fusion(bf16[25,32,256]{1,0,2:T(8,128)(2,1)S(1)} %get-tuple-element.574, s32[2048]{0:T(1024)S(1)} %bitcast_clamp_fusion.4), kind=kCustom, calls=%fused_computation.2.clone.clone.1 | custom fusion | bytes 6561792 | tf_op jit(solution)/shard_map/while/body/eval_jaxpr/jit(_take)/gather | solution.py:64
  409.1 14.9 %copy.110 = bf16[16,128,25,32]{1,0,3,2:T(8,128)(2,1)} copy(bf16[16,128,25,32]{3,2,1,0:T(8,128)(2,1)} %bitcast.209) | data formatting | bytes 6553600 | tf_op jit(solution)/shard_map/while/body/eval_jaxpr/jit(_take)/gather | solution.py:64
  424.0 3.6 fusion.93
  427.6 2.9 copy.54
  431.3 12.3 %all_gather.6 = bf16[128,1024]{1,0:T(8,128)(2,1)S(1)} all-gather(bf16[32,1024]{1,0:T(8,128)(2,1)S(1)} %multiply_reduce_fusion), channel_id=1, replica_groups=mesh['cells'=64,'chan'=4] {'chan'}, dimensions={0}, use_global_device_ids=true | all-gather | bytes 327680 | tf_op jit(solution)/shard_map/all_gather | solution.py:146
  443.6 48.4 %all-reduce.7.cloned.1.call-done = (f32[25,25,64]{1,2,0:T(8,128)}, f32[25,25,64]{1,2,0:T(8,128)}) async-done(((f32[25,25,64]{1,2,0:T(8,128)}, f32[25,25,64]{1,2,0:T(8,128)}), (f32[25,25,64]{1,2,0:T(8,128)}, f32[25,25,64]{1,2,0:T(8,128)})) %all-reduce.7.cloned.1.call-update) | async-done | bytes 320016 | tf_op jit(solution)/shard_map/psum | solution.py:164
  492.0 0.9 fusion.52
  492.9 190.3 %all-reduce.5.cloned.1.call-done = (f32[25,25,64]{1,2,0:T(8,128)}, f32[25,25,64]{1,2,0:T(8,128)}) async-done(((f32[25,25,64]{1,2,0:T(8,128)}, f32[25,25,64]{1,2,0:T(8,128)}), (f32[25,25,64]{1,2,0:T(8,128)}, f32[25,25,64]{1,2,0:T(8,128)})) %all-reduce.5.cloned.1.call-update) | async-done | bytes 320016 | tf_op jit(solution)/shard_map/psum | solution.py:164
  683.2 2.2 copy.62
  685.5 2.2 copy.63
  (139 shorter events, 19.3 us)
Async XLA Ops:
  7.2 28.6 %copy-start = (bf16[128,128]{1,0:T(8,128)(2,1)S(1)}, bf16[128,128]{1,0:T(8,128)(2,1)}, u32[]{:S(2)}) copy-start(bf16[128,128]{1,0:T(8,128)(2,1)} %param.32) | copy-start | bytes 98308
  7.2 484.8 %all-reduce.7.cloned.1.call-start = ((), (), s32[]{:S(2)}) async-start(), calls=%async_computation.1 | async-start | bytes 3276800 | tf_op jit(solution)/shard_map/psum | solution.py:164
  8.1 9.2 %copy-start.8 = (bf16[8,25,25]{2,0,1:T(8,128)(2,1)S(1)}, bf16[8,25,25]{2,0,1:T(8,128)(2,1)}, u32[]{:S(2)}) copy-start(bf16[8,25,25]{2,0,1:T(8,128)(2,1)} %param.28) | copy-start | bytes 30004
  8.8 27.1 %copy-start.12 = (s32[1024]{0:T(1024)}, s32[1024]{0:T(1024)S(1)}, u32[]{:S(2)}) copy-start(s32[1024]{0:T(1024)S(1)} %broadcast_subtract_fusion) | copy-start | bytes 12292
  10.4 13.0 %copy-start.10 = (bf16[32,1024]{1,0:T(8,128)(2,1)S(1)}, bf16[32,1024]{1,0:T(8,128)(2,1)}, u32[]{:S(2)}) copy-start(bf16[32,1024]{1,0:T(8,128)(2,1)} %param.33) | copy-start | bytes 196612
  10.4 25.5 %copy-start.14 = (f32[25,1024]{1,0:T(8,128)S(1)}, f32[25,1024]{1,0:T(8,128)}, u32[]{:S(2)}) copy-start(f32[25,1024]{1,0:T(8,128)} %param.24) | copy-start | bytes 307204
  11.3 67.6 %collective-permute-start.1 = (bf16[25,32,64]{2,1,0:T(8,128)(2,1)}, bf16[25,32,64]{2,1,0:T(8,128)(2,1)}, u32[]{:S(2)}, u32[]{:S(2)}) collective-permute-start(bf16[25,32,64]{2,1,0:T(8,128)(2,1)} %get-tuple-element.333), channel_id=1, source_target_pairs={{4,0},{8,4},{12,8},{16,12},{20,16},{24,20},{28,24},{32,28},{36,32}... | collective-permute-start | bytes 307208 | tf_op jit(solution)/shard_map/ppermute | solution.py:17
  13.2 65.6 %collective-permute-start = (bf16[25,32,64]{2,1,0:T(8,128)(2,1)}, bf16[25,32,64]{2,1,0:T(8,128)(2,1)}, u32[]{:S(2)}, u32[]{:S(2)}) collective-permute-start(bf16[25,32,64]{2,1,0:T(8,128)(2,1)} %get-tuple-element.332), channel_id=1, source_target_pairs={{0,4},{4,8},{8,12},{12,16},{16,20},{20,24},{24,28},{28,32},{32,36}... | collective-permute-start | bytes 307208 | tf_op jit(solution)/shard_map/ppermute | solution.py:14
  17.7 20.7 %copy-start.9 = (bf16[8,25,25]{2,0,1:T(8,128)(2,1)S(1)}, bf16[8,25,25]{2,0,1:T(8,128)(2,1)}, u32[]{:S(2)}) copy-start(bf16[8,25,25]{2,0,1:T(8,128)(2,1)} %param.29) | copy-start | bytes 30004
  17.7 25.4 %collective-permute-start.3 = (bf16[25,32,8]{0,1,2:T(8,128)(2,1)S(1)}, bf16[25,32,8]{0,1,2:T(8,128)(2,1)S(1)}, u32[]{:S(2)}, u32[]{:S(2)}) collective-permute-start(bf16[25,32,8]{0,1,2:T(8,128)(2,1)S(1)} %get-tuple-element.335), channel_id=1, source_target_pairs={{4,0},{8,4},{12,8},{16,12},{20,16},{24,20},{28,24},{32,28},{36,32}... | collective-permute-start | bytes 38408 | tf_op jit(solution)/shard_map/ppermute | solution.py:17
  21.5 21.6 %collective-permute-start.2 = (bf16[25,32,8]{0,1,2:T(8,128)(2,1)S(1)}, bf16[25,32,8]{0,1,2:T(8,128)(2,1)S(1)}, u32[]{:S(2)}, u32[]{:S(2)}) collective-permute-start(bf16[25,32,8]{0,1,2:T(8,128)(2,1)S(1)} %get-tuple-element.334), channel_id=1, source_target_pairs={{0,4},{4,8},{8,12},{12,16},{16,20},{20,24},{24,28},{28,32},{32,36}... | collective-permute-start | bytes 38408 | tf_op jit(solution)/shard_map/ppermute | solution.py:14
  35.9 3.6 copy-start.5
  36.6 4.6 copy-start.6
  36.7 5.5 copy-start.11
  58.4 0.9 copy-start.7
  62.8 0.9 copy-start.7
  67.1 0.9 copy-start.7
  71.5 0.9 copy-start.7
  78.8 4.3 copy-start.1
  83.1 193.5 %copy-start.3 = (bf16[25,32,128]{2,0,1:T(8,128)(2,1)S(1)}, bf16[25,32,128]{2,0,1:T(8,128)(2,1)}, u32[]{:S(2)}) copy-start(bf16[25,32,128]{2,0,1:T(8,128)(2,1)} %copy.53) | copy-start | bytes 614404
  427.5 3.0 copy-start.2
  427.5 3.1 copy-start.13
  427.6 3.1 copy-start.15
  430.5 252.7 %all-reduce.5.cloned.1.call-start = ((), (), s32[]{:S(2)}) async-start(), calls=%async_computation | async-start | bytes 3276800 | tf_op jit(solution)/shard_map/psum | solution.py:164
  430.7 61.3 %copy-start.4 = (bf16[32,1024]{1,0:T(8,128)(2,1)S(1)}, bf16[32,1024]{1,0:T(8,128)(2,1)}, u32[]{:S(2)}) copy-start(bf16[32,1024]{1,0:T(8,128)(2,1)} %param.23) | copy-start | bytes 196612
Sparse Core Ops, SparseCore 0:
  430.6 61.2 all-reduce.6
  495.5 187.7 all-reduce.4
